TPU v7x, 512 devices: a whole 4x8x8 slice. The times are simulated.
512 devices in a mesh: rows: 64 (over x, y, z_lo), cols: 8 (over z_hi, core).
Axes of the slice: x: 4, y: 8, z: 8 (z_hi: 4, z_lo: 2; z = z_hi * 2 + z_lo), core: 2. Of those that a mesh axis runs over, the one named last changes fastest.
Arguments:
- design: float32 [65536, 4096], P('rows', 'cols')
- signs: int32 [65536], P('rows'), may hold values from -1 to 1, as said below
- response: float32 [65536], P('rows'), may hold values from -6 to 6
- picks: int32 [8192], replicated, may hold values from 0 to 65535, as said below
Outputs:
- gram_blocks: float32 [512, 8, 512], P('rows', 'cols')
- rhs: float32 [4096], P('cols')
Inputs may be any that keep to these rules, and one draw needn't show every extreme that they name: `signs`: every entry is +1 or -1. `picks`: strictly increasing, all distinct; the first and the last row are always sampled.
All inputs are finite; a program needn't handle non-finite values.
Results may differ from a plain program's by a relative error of at most 0.0003.
Values sent between devices are 32-bit elements; how exact they have to be, the bound alone decides.
A program may use at most 64 MiB of HBM per device.

v0:
```python
import jax
import jax.numpy as jnp
from jax import lax
from jax.sharding import PartitionSpec as P

D = 4096
BW = 512
epsilon = 1e-06


def sylvester(order, dtype):
    row_ids = lax.broadcasted_iota(jnp.int32, (order, order), 0)
    col_ids = lax.broadcasted_iota(jnp.int32, (order, order), 1)
    common = jnp.bitwise_and(row_ids, col_ids)
    return (1 - 2 * jnp.bitwise_and(lax.population_count(common), 1)).astype(dtype)


def halves(values):
    top = lax.reduce_precision(values, 8, 7)
    rest = values - top
    return (top.astype(jnp.bfloat16), rest.astype(jnp.bfloat16))


def thirds(values):
    top = lax.reduce_precision(values, 8, 7)
    rest = values - top
    mid = lax.reduce_precision(rest, 8, 7)
    low = rest - mid
    return tuple((part.astype(jnp.bfloat16) for part in (top, mid, low)))


def dot(left, right):
    return jnp.dot(left, right, preferred_element_type=jnp.float32)


def mix(order, values):
    matrix = sylvester(order, jnp.bfloat16)
    return sum((dot(matrix, part) for part in halves(values)))


def local(design, signs, response, picks):
    height, width = design.shape
    groups = lax.axis_size("rows")
    position = lax.axis_index("rows")
    share = height // groups
    flips = signs.astype(jnp.float32)
    whole = lax.all_gather(response * flips, "rows", axis=0, tiled=True)
    side = 256
    square = whole.reshape(side, side)
    h_side = sylvester(side, jnp.bfloat16)
    square = sum((dot(h_side, part) for part in thirds(square)))
    square = sum((dot(part, h_side) for part in thirds(square)))
    answer = square.reshape(groups, groups, share)
    answer = lax.dynamic_slice_in_dim(answer, position, 1, axis=1)[:, 0, :]
    mixed = mix(height, design * flips[:, None])
    mixed = lax.all_to_all(
        mixed.reshape(groups, share, width), "rows", split_axis=0, concat_axis=0, tiled=True
    )
    mixed = mix(groups, mixed.reshape(groups, share * width)).reshape(height, width)
    group_of = picks // height
    inside = picks % height - position * share
    of_group = (lax.iota(jnp.int32, groups)[:, None] == group_of[None, :]).astype(jnp.bfloat16)
    of_local = (inside[:, None] == lax.iota(jnp.int32, share)[None, :]).astype(jnp.bfloat16)
    picked = dot(of_group, of_local)
    picked_answer = picked * answer
    chosen = mixed * picked.reshape(height)[:, None]
    top, rest = halves(chosen)

    def outer(left, right):
        return lax.dot_general(
            left, right, (((0,), (0,)), ((), ())), preferred_element_type=jnp.float32
        )

    cross = outer(top, rest)
    gram = outer(top, top) + cross + cross.T
    rhs_part = jnp.sum(chosen * picked_answer.reshape(height)[:, None], axis=0)
    power_part = jnp.sum(picked_answer * picked_answer)
    trace_part = jnp.sum(chosen * chosen)
    trace_sum = lax.psum(trace_part, ("rows", "cols"))
    blocks = gram.reshape(groups, BW // groups, width)
    extra = jnp.stack([rhs_part, jnp.full((width,), power_part)])
    extra = jnp.broadcast_to(extra[None], (groups, 2, width))
    parts = jnp.concatenate([blocks, extra], axis=1)
    parts = lax.all_to_all(parts, "rows", split_axis=0, concat_axis=0, tiled=True)
    sums = jnp.sum(parts, axis=0)
    mean_diag = trace_sum / D + epsilon
    gram_blocks = sums[: BW // groups, None, :] / mean_diag
    samples = picks.shape[0]
    rhs = (
        sums[BW // groups]
        * jnp.sqrt(jnp.float32(samples))
        / jnp.sqrt(mean_diag * sums[BW // groups + 1])
    )
    return (gram_blocks, rhs)


def solution(mesh):
    in_specs = (P("rows", "cols"), P("rows"), P("rows"), P())
    out_specs = (P("rows", "cols", None), P("cols"))
    return jax.shard_map(local, mesh=mesh, in_specs=in_specs, out_specs=out_specs, check_vma=False)
```

profile of v0, /device:TPU:27, one launch (start us, length us, event | category | flops | bytes accessed | tf_op | source)
XLA Modules:
  0.0 366.3 jit_solution(7511353022532499297)
XLA Ops:
  0.6 0.7 convert_element_type.74
  1.3 3.2 fusion.3
  4.5 2.7 fusion.6
  7.2 11.7 %all-to-all-start = ((f32[64,16,512]{2,1,0:T(8,128)}), f32[64,16,512]{2,1,0:T(8,128)S(1)}, u32[]{:S(2)}, u32[]{:S(2)}) async-start(f32[64,16,512]{2,1,0:T(8,128)} %bitcast.23), calls=%async_computation | async-start | bytes 4194304 | tf_op jit(solution)/shard_map/all_to_all | solution.py:56
  19.0 136.0 %all_gather.3 = f32[65536]{0:T(1024)S(1)} all-gather(f32[1024]{0:T(1024)S(1)} %convert_multiply_fusion), channel_id=1, replica_groups=mesh['rows'=64,'cols'=8] {'rows'}, dimensions={0}, use_global_device_ids=true | all-gather | bytes 266240 | tf_op jit(solution)/shard_map/all_gather | solution.py:47
  156.4 2.0 reshape.59
  158.4 1.0 constant_dynamic-slice_fusion
  159.4 1.1 multiply_reduce_fusion.2
  161.1 2.5 copy.25
  163.6 1.2 copy.24
  165.2 1.2 copy-done
  166.4 2.7 multiply_reduce_fusion
  169.1 1.3 convert_element_type.82
  170.4 0.5 convert_element_type.80
  170.9 2.0 fusion.47
  172.9 1.3 copy.20
  174.2 2.0 fusion.8
  176.2 1.8 reshape.57
  178.3 0.7 stack.7
  179.0 1.6 pad_maximum_fusion
  180.7 32.6 %all-to-all-start.1 = ((f32[64,10,512]{2,1,0:T(8,128)}), f32[64,10,512]{2,1,0:T(8,128)S(1)}, u32[]{:S(2)}, u32[]{:S(2)}) async-start(f32[64,10,512]{2,1,0:T(8,128)} %pad_maximum_fusion), calls=%async_computation.1 | async-start | bytes 4194304 | tf_op jit(solution)/shard_map/all_to_all | solution.py:84
  213.3 150.9 %psum.7 = f32[]{:T(128)} all-reduce(f32[]{:T(128)} %get-tuple-element.4), channel_id=1, replica_groups=mesh['rows'=64,'cols'=8] {'rows','cols'}, use_global_device_ids=true, to_apply=%region_4.5 | all-reduce | flops 1 | bytes 8 | tf_op jit(solution)/shard_map/psum | solution.py:79
  365.1 0.6 fusion.26
  365.6 0.6 div.36
  (31 shorter events, 3.0 us)
Async XLA Ops:
  1.3 3.2 copy-start.4
  7.2 11.7 %copy-start.2 = (s32[1024]{0:T(1024)S(1)}, s32[1024]{0:T(1024)}, u32[]{:S(2)}) copy-start(s32[1024]{0:T(1024)} %param.5) | copy-start | bytes 12292
  7.2 11.8 %copy-start.3 = (f32[1024]{0:T(1024)S(1)}, f32[1024]{0:T(1024)}, u32[]{:S(2)}) copy-start(f32[1024]{0:T(1024)} %param.6) | copy-start | bytes 12292
  7.2 156.3 %all-to-all-start = ((f32[64,16,512]{2,1,0:T(8,128)}), f32[64,16,512]{2,1,0:T(8,128)S(1)}, u32[]{:S(2)}, u32[]{:S(2)}) async-start(f32[64,16,512]{2,1,0:T(8,128)} %bitcast.23), calls=%async_computation | async-start | bytes 4194304 | tf_op jit(solution)/shard_map/all_to_all | solution.py:56
  155.9 3.5 copy-start.1
  164.8 1.6 copy-start
  180.7 184.2 %all-to-all-start.1 = ((f32[64,10,512]{2,1,0:T(8,128)}), f32[64,10,512]{2,1,0:T(8,128)S(1)}, u32[]{:S(2)}, u32[]{:S(2)}) async-start(f32[64,10,512]{2,1,0:T(8,128)} %pad_maximum_fusion), calls=%async_computation.1 | async-start | bytes 4194304 | tf_op jit(solution)/shard_map/all_to_all | solution.py:84
where the time goes:
time: 367 us; the launch traced here: 366 us
  blocking collectives  287 us (78%)
  starting transfers between devices  44.3 us (12%)
  matrix products  15.4 us (4%)
  local copies, waits for them, and re-layouts  14.7 us (4%)
    psum x1, blocking collectives, local(): trace_sum = lax.psum(trace_part, ('rows', 'cols'))  151 us
    all_gather x1, blocking collectives, local(): whole = lax.all_gather(response * flips, 'rows', axis=0, tiled=True)  136 us
    all_to_all x1, starting transfers between devices, local(): lax.all_to_all(parts, 'rows', split_axis=0, concat_axis=0, tiled=True)  32.6 us
    all_to_all x1, starting transfers between devices, local(): lax.all_to_all(mixed.reshape(groups, share, width), 'rows', split_axis=0,...  11.7 us
    dot_general x11, matrix products, dot(): return jnp.dot(left, right, preferred_element_type=jnp.float32)  11.4 us
  transfers between devices with their start and end apart: 2, of which 0 were waited for; matrix products, arithmetic and copies ran while one was open for 2% of the time, Pallas kernels for 0%

commit v1 on v0

--- a/solution.py
+++ b/solution.py
@@ -44,7 +44,9 @@
     position = lax.axis_index("rows")
     share = height // groups
     flips = signs.astype(jnp.float32)
-    whole = lax.all_gather(response * flips, "rows", axis=0, tiled=True)
+    whole = jnp.concatenate(
+        lax.all_to_all(jnp.stack([response * flips] * lax.axis_size("rows")), "rows", 0, 0), axis=0
+    )
     side = 256
     square = whole.reshape(side, side)
     h_side = sylvester(side, jnp.bfloat16)

time: 367 us -> 252 us (0.69)
  blocking collectives: 287 us -> 144 us
  waiting for transfers between devices: 0.01 us -> 40.3 us
  starting transfers between devices: 44.3 us -> 29.8 us
    all_gather x1 -> x0, blocking collectives: 136 us -> none  [local(): whole = lax.all_gather(response * flips, 'rows', axis=0, tiled=True)]
    all_to_all x1, waiting for transfers between devices: 0.01 us -> 37.8 us  [local(): lax.all_to_all(mixed.reshape(groups, share, width), 'rows', split_axis=0,...]
    all_to_all x1, starting transfers between devices: 32.6 us -> 9.66 us  [local(): lax.all_to_all(parts, 'rows', split_axis=0, concat_axis=0, tiled=True)]
    all_to_all x0 -> x1, starting transfers between devices: none -> 11.6 us  [local(): lax.all_to_all(jnp.stack([response * flips] * lax.axis_size('rows')), 'ro...]
    psum x1, blocking collectives: 151 us -> 144 us  [local(): trace_sum = lax.psum(trace_part, ('rows', 'cols'))]
  transfers between devices with their start and end apart: 2 -> 3, of which waited for: 0 -> 2; matrix products, arithmetic and copies ran while one was open for 2% -> 6% of each run, Pallas kernels for 0% -> 0%
where the time goes in v1:
time: 252 us; the launch traced here: 251 us
  blocking collectives  144 us (57%)
  waiting for transfers between devices  40.3 us (16%)
  starting transfers between devices  29.8 us (12%)
  local copies, waits for them, and re-layouts  15.5 us (6%)
  matrix products  15.4 us (6%)
  other arithmetic  4.8 us (2%)
    psum x1, blocking collectives, local(): trace_sum = lax.psum(trace_part, ('rows', 'cols'))  144 us
    all_to_all x1, waiting for transfers between devices, local(): lax.all_to_all(mixed.reshape(groups, share, width), 'rows', split_axis=0,...  37.8 us
    all_to_all x1, starting transfers between devices, local(): lax.all_to_all(jnp.stack([response * flips] * lax.axis_size('rows')), 'ro...  11.6 us
    dot_general x11, matrix products, dot(): return jnp.dot(left, right, preferred_element_type=jnp.float32)  11.5 us
    all_to_all x1, starting transfers between devices, local(): lax.all_to_all(parts, 'rows', split_axis=0, concat_axis=0, tiled=True)  9.66 us
    all_to_all x1, starting transfers between devices, local(): lax.all_to_all(mixed.reshape(groups, share, width), 'rows', split_axis=0,...  8.53 us
  transfers between devices with their start and end apart: 3, of which 2 were waited for; matrix products, arithmetic and copies ran while one was open for 6% of the time, Pallas kernels for 0%

profile of v1, /device:TPU:27, one launch (start us, length us, event | category | flops | bytes accessed | tf_op | source)
XLA Modules:
  0.0 250.9 jit_solution(13751477860775774677)
XLA Ops:
  0.6 0.7 convert_multiply_fusion
  1.3 0.9 stack.6
  2.2 11.6 %all-to-all-start.1 = ((f32[64,1,1024]{2,1,0:T(1,128)}), f32[64,1,1024]{2,1,0:T(1,128)S(1)}, u32[]{:S(2)}, u32[]{:S(2)}) async-start(f32[64,1,1024]{2,1,0:T(1,128)} %stack.6), calls=%async_computation.1 | async-start | bytes 524288 | tf_op jit(solution)/shard_map/all_to_all | solution.py:48
  13.8 0.7 convert_element_type.74
  14.5 3.2 %fusion.3 = f32[1024,512]{1,0:T(8,128)S(1)} fusion(f32[1024,512]{1,0:T(8,128)} %param.4, f32[1024]{0:T(1024)S(1)} %convert_element_type.74), kind=kOutput, calls=%fused_computation.15 | convolution fusion | flops 1082130432 | bytes 4198400 | tf_op jit(solution)/shard_map/dot_general | solution.py:33
  17.7 2.7 %fusion.6 = f32[1024,512]{1,0:T(8,128)} fusion(f32[1024,512]{1,0:T(8,128)S(1)} %fusion.3, f32[1024,512]{1,0:T(8,128)S(1)} %copy-done.2, f32[1024]{0:T(1024)S(1)} %convert_element_type.74), kind=kOutput, calls=%fused_computation.18 | convolution fusion | flops 1082130432 | bytes 6295552 | tf_op jit(solution)/shard_map/dot_general | solution.py:33
  20.4 2.6 %all-to-all-done.1 = f32[64,1,1024]{2,1,0:T(1,128)S(1)} async-done(((f32[64,1,1024]{2,1,0:T(1,128)}), f32[64,1,1024]{2,1,0:T(1,128)S(1)}, u32[]{:S(2)}, u32[]{:S(2)}) %all-to-all-start.1) | async-done | bytes 262176 | tf_op jit(solution)/shard_map/all_to_all | solution.py:48
  23.0 8.5 %all-to-all-start = ((f32[64,16,512]{2,1,0:T(8,128)}), f32[64,16,512]{2,1,0:T(8,128)S(1)}, u32[]{:S(2)}, u32[]{:S(2)}) async-start(f32[64,16,512]{2,1,0:T(8,128)} %bitcast.23), calls=%async_computation | async-start | bytes 4194304 | tf_op jit(solution)/shard_map/all_to_all | solution.py:58
  33.6 2.0 reshape.63
  35.6 1.0 constant_dynamic-slice_fusion
  36.6 1.1 multiply_reduce_fusion.2
  38.2 2.5 copy.20
  40.7 37.8 %all-to-all-done = f32[64,16,512]{2,1,0:T(8,128)S(1)} async-done(((f32[64,16,512]{2,1,0:T(8,128)}), f32[64,16,512]{2,1,0:T(8,128)S(1)}, u32[]{:S(2)}, u32[]{:S(2)}) %all-to-all-start) | async-done | bytes 2097184 | tf_op jit(solution)/shard_map/all_to_all | solution.py:58
  78.5 1.2 copy.19
  80.1 1.2 copy-done
  81.3 2.7 %multiply_reduce_fusion = (f32[]{:T(128)}, bf16[64,8192]{1,0:T(8,128)(2,1)S(1)}, bf16[64,8192]{1,0:T(8,128)(2,1)S(1)}, f32[64,8192]{1,0:T(8,128)}) fusion(f32[64,8192]{1,0:T(8,128)S(1)} %bitcast.22, f32[64,8192]{1,0:T(8,128)S(1)} %fusion.11, f32[64,8192]{1,0:T(8,128)S(1)} %bitcast.19), kind=kOutput, calls=%fused_computation.12 | convolution fusion | flops 72900608 | bytes 10485764 | tf_op jit(solution)/shard_map/dot_general | solution.py:33
  84.0 1.3 convert_element_type.82
  85.8 2.0 fusion.47
  87.8 1.3 copy.15
  89.1 2.0 fusion.8
  91.1 1.8 reshape.62
  94.0 1.6 pad_maximum_fusion
  95.6 9.7 %all-to-all-start.2 = ((f32[64,10,512]{2,1,0:T(8,128)}), f32[64,10,512]{2,1,0:T(8,128)S(1)}, u32[]{:S(2)}, u32[]{:S(2)}) async-start(f32[64,10,512]{2,1,0:T(8,128)} %pad_maximum_fusion), calls=%async_computation.2 | async-start | bytes 4194304 | tf_op jit(solution)/shard_map/all_to_all | solution.py:86
  105.3 143.6 %psum.7 = f32[]{:T(128)} all-reduce(f32[]{:T(128)} %get-tuple-element.4), channel_id=1, replica_groups=mesh['rows'=64,'cols'=8] {'rows','cols'}, use_global_device_ids=true, to_apply=%region_4.5 | all-reduce | flops 1 | bytes 8 | tf_op jit(solution)/shard_map/psum | solution.py:81
  (30 shorter events, 6.0 us)
Async XLA Ops:
  2.2 20.8 %all-to-all-start.1 = ((f32[64,1,1024]{2,1,0:T(1,128)}), f32[64,1,1024]{2,1,0:T(1,128)S(1)}, u32[]{:S(2)}, u32[]{:S(2)}) async-start(f32[64,1,1024]{2,1,0:T(1,128)} %stack.6), calls=%async_computation.1 | async-start | bytes 524288 | tf_op jit(solution)/shard_map/all_to_all | solution.py:48
  14.5 3.2 %copy-start.2 = (f32[1024,512]{1,0:T(8,128)S(1)}, f32[1024,512]{1,0:T(8,128)}, u32[]{:S(2)}) copy-start(f32[1024,512]{1,0:T(8,128)} %param.4) | copy-start | bytes 6291460
  23.0 8.5 %copy-start.1 = (s32[8192]{0:T(1024)S(1)}, s32[8192]{0:T(1024)}, u32[]{:S(2)}) copy-start(s32[8192]{0:T(1024)} %param.7) | copy-start | bytes 98308
  23.0 55.5 %all-to-all-start = ((f32[64,16,512]{2,1,0:T(8,128)}), f32[64,16,512]{2,1,0:T(8,128)S(1)}, u32[]{:S(2)}, u32[]{:S(2)}) async-start(f32[64,16,512]{2,1,0:T(8,128)} %bitcast.23), calls=%async_computation | async-start | bytes 4194304 | tf_op jit(solution)/shard_map/all_to_all | solution.py:58
  79.7 1.6 copy-start
  95.6 153.9 %all-to-all-start.2 = ((f32[64,10,512]{2,1,0:T(8,128)}), f32[64,10,512]{2,1,0:T(8,128)S(1)}, u32[]{:S(2)}, u32[]{:S(2)}) async-start(f32[64,10,512]{2,1,0:T(8,128)} %pad_maximum_fusion), calls=%async_computation.2 | async-start | bytes 4194304 | tf_op jit(solution)/shard_map/all_to_all | solution.py:86
